TPU v7x, 32 devices: a whole 2x2x4 slice. The times are simulated.
32 devices in a mesh: grp: 2 (over y), ka: 4 (over z), ga: 2 (over x), ba: 2 (over core).
Axes of the slice: x: 2, y: 2, z: 4, core: 2. Of those that a mesh axis runs over, the one named last changes fastest.
Arguments:
- coefficients: bfloat16 [2, 2, 16, 512, 9216], P(None, None, ('grp', 'ka'), 'ba', 'ga'), parts along dimension 2, may hold values from -1 to 1
- occupied: int32 [2, 16], P(None, ('grp', 'ka')), parts along dimension 1, may hold values from 64 to 512
- kweights: float32 [16], P(('grp', 'ka')), parts along dimension 0, may hold values from 0.5 to 2
- owner_map: int32 [1024], P('grp'), parts along dimension 0, may hold values from 0 to 7, as said below
- species: int32 [1024], P('grp'), parts along dimension 0, may hold values from 0 to 1
- positions: float32 [3, 1024], P(None, 'grp'), parts along dimension 1, may hold values from 0 to 100
- multipole: float32 [2, 9, 324], replicated, may hold values from -0.3125 to 0.3125
- widths: float32 [2], replicated, may hold values from 0.05 to 0.3
- potential: float32 [2, 442368], P(None, ('grp', 'ga')), parts along dimension 1, may hold values from -0.013671875 to 0.013671875
Outputs:
- density: float32 [2, 2, 1024, 324], P(None, None, ('grp', 'ka', 'ga', 'ba')), parts along dimension 2
- forces: float32 [3, 1024], P(None, ('grp', 'ka', 'ga', 'ba')), parts along dimension 1
There are 2 independent parts, one for each index of `grp`. A program takes and returns all parts, laid end to end along the dimension named above; an argument that names none is the same for every part. Nothing has to cross between parts.
Inputs may be any that keep to these rules, and one draw needn't show every extreme that they name: `owner_map`: within each aligned block of 256 atoms every owner number is named by exactly 32 atoms.
All inputs are finite; a program needn't handle non-finite values.
Results may differ from a plain program's by a relative error of at most 0.0003.
Values sent between devices are 32-bit elements; how exact they have to be, the bound alone decides.
A program may use at most 192 MiB of HBM per device.

v0:
```python
import jax
import jax.numpy as jnp
from jax import lax
from jax.sharding import PartitionSpec as P

NPROJ = 18
SPECIES = 2
NL = 9
GRID = 96
grid_step = 0.0625
highest = lax.Precision.HIGHEST


def harmonics(start_index, length, widths):
    indices = start_index + jnp.arange(length, dtype=jnp.int32)
    planes = [indices % GRID, indices // GRID % GRID, indices // (GRID * GRID)]
    vectors = []
    for plane_index in planes:
        signed = jnp.where(plane_index >= GRID // 2, plane_index - GRID, plane_index)
        vectors.append(grid_step * signed.astype(jnp.float32))
    along_x, along_y, along_z = vectors
    square = along_x * along_x + along_y * along_y + along_z * along_z
    shapes = jnp.stack(
        [
            jnp.ones_like(square),
            along_x,
            along_y,
            along_z,
            along_x * along_y,
            along_y * along_z,
            along_z * along_x,
            along_x * along_x - along_y * along_y,
            3.0 * along_z * along_z - square,
        ]
    )
    damping = jnp.exp(-widths[:, None] * square[None, :])
    form_table = (damping[:, None, :] * shapes[None, :, :]).reshape(SPECIES * NL, length)
    return (form_table, jnp.stack(vectors, axis=1))


def force_block(moments, places, form_table, vectors, pot_piece):
    smooth = jnp.dot(moments, form_table, precision=highest)
    phases = jnp.dot(places, vectors.T, precision=highest)
    wave_term = pot_piece[0][None, :] * jnp.sin(phases) + pot_piece[1][None, :] * jnp.cos(phases)
    return jnp.dot(smooth * wave_term, vectors, precision=highest)


def local_force(moments, places, pot_piece, start_index, widths):
    length = pot_piece.shape[1]
    pieces = 8
    width_block = length // pieces

    def gblock(running, number):
        offset = number * width_block
        form_table, vectors = harmonics(start_index + offset, width_block, widths)
        segment = lax.dynamic_slice_in_dim(pot_piece, offset, width_block, 1)
        return (running + force_block(moments, places, form_table, vectors, segment), None)

    result, unused = lax.scan(
        gblock, jnp.zeros((moments.shape[0], 3), jnp.float32), jnp.arange(pieces, dtype=jnp.int32)
    )
    return result


def shards(
    coefficients, occupied, kweights, owner_map, species, positions, multipole, widths, potential
):
    spin_count, complex_parts, kcount, bcount, columns = coefficients.shape
    atoms_blk = columns // NPROJ
    kgroups = lax.axis_size("ka")
    bgroups = lax.axis_size("ba")
    owners = kgroups * bgroups
    per_owner = atoms_blk // owners
    owner_index = lax.axis_index(("ka", "ba"))
    group_index = lax.axis_index("ga")
    band_index = lax.axis_index("ba") * bcount + jnp.arange(bcount, dtype=jnp.int32)
    band_mask = (band_index[None, None, :] < occupied[:, :, None]).astype(jnp.bfloat16)
    values = coefficients.reshape(spin_count, complex_parts, kcount, bcount, atoms_blk, NPROJ)
    masked = values * band_mask[:, None, :, :, None, None]
    real_part = jnp.einsum(
        "sckbai,sckbaj->skaij", values, masked, preferred_element_type=jnp.float32
    )
    cross_term = jnp.einsum(
        "skbai,skbaj->skaij", values[:, 0], masked[:, 1], preferred_element_type=jnp.float32
    )
    imag_part = cross_term - jnp.swapaxes(cross_term, 3, 4)
    weighted = jnp.stack([real_part, imag_part], axis=1) * kweights[None, None, :, None, None, None]
    density_local = jnp.sum(weighted, axis=2).reshape(
        spin_count, complex_parts, atoms_blk, NPROJ * NPROJ
    )
    ranking = jnp.argsort(owner_map.reshape(-1, atoms_blk), axis=1, stable=True)
    own_ranks = lax.dynamic_slice_in_dim(ranking, owner_index * per_owner, per_owner, 1)
    summed = lax.psum(density_local, ("ka", "ba"))
    own_rows = lax.dynamic_index_in_dim(own_ranks, group_index, 0, keepdims=False)
    own_density = jnp.take(summed, own_rows, axis=2)
    block_count = own_ranks.shape[0]
    atom_ids = jnp.arange(block_count, dtype=jnp.int32)[:, None] * atoms_blk + own_ranks
    own_atoms = lax.dynamic_index_in_dim(atom_ids, group_index, 0, keepdims=False)
    real_total = jnp.sum(own_density[:, 0], axis=0)
    selector = (
        jnp.take(species, own_atoms)[:, None] == jnp.arange(SPECIES, dtype=jnp.int32)[None, :]
    ).astype(jnp.float32)
    moments = jnp.dot(
        real_total, multipole.reshape(SPECIES * NL, NPROJ * NPROJ).T, precision=highest
    ) * jnp.repeat(selector, NL, axis=1)
    gcount = potential.shape[1]
    all_moments = lax.all_gather(moments, "ga", axis=0, tiled=True)
    places = jnp.take(positions, atom_ids.reshape(-1), axis=1).T
    partial_force = local_force(all_moments, places, potential, group_index * gcount, widths)
    summed_force = lax.psum(partial_force, "ga")
    own_force = lax.dynamic_slice_in_dim(summed_force, group_index * per_owner, per_owner, 0)
    return (own_density, own_force.T)


def solution(mesh):
    placed = (
        P(None, None, ("grp", "ka"), "ba", "ga"),
        P(None, ("grp", "ka")),
        P(("grp", "ka")),
        P("grp"),
        P("grp"),
        P(None, "grp"),
        P(),
        P(),
        P(None, ("grp", "ga")),
    )
    return jax.shard_map(
        shards,
        mesh=mesh,
        in_specs=placed,
        out_specs=(
            P(None, None, ("grp", "ka", "ga", "ba"), None),
            P(None, ("grp", "ka", "ga", "ba")),
        ),
        check_vma=False,
    )
```

profile of v0, /device:TPU:0, one launch (start us, length us, event | category | flops | bytes accessed | tf_op | source)
XLA Modules:
  0.0 663.2 jit_solution(12733213700706561287)
XLA Ops:
  8.1 1.3 reshape.503
  10.0 45.7 %copy.45 = bf16[2,2,2,256,4608]{3,2,4,1,0:T(2,128)(2,1)} copy(bf16[2,2,2,256,4608]{4,3,2,1,0:T(8,128)(2,1)} %param.11) | data formatting | bytes 37748736 | tf_op args[0]
  55.7 45.4 %copy.46 = bf16[2,2,2,256,256,18]{4,3,5,2,1,0:T(8,128)(2,1)} copy(bf16[2,2,2,256,256,18]{3,2,5,4,1,0:T(2,128)(2,1)} %bitcast.68) | data formatting | bytes 37748736 | tf_op jit(solution)/shard_map/reshape | solution.py:78
  101.1 9.1 %slice.35 = bf16[2,1,2,256,256,18]{3,2,5,4,1,0:T(2,128)(2,1)} slice(bf16[2,2,2,256,256,18]{3,2,5,4,1,0:T(2,128)(2,1)} %bitcast.69), slice={[0:2], [0:1], [0:2], [0:256], [0:256], [0:18]} | slice | bytes 18874368 | tf_op jit(solution)/shard_map/slice | solution.py:84
  110.3 16.7 %broadcast_multiply_fusion.2 = bf16[2,2,2,256,256,18]{4,3,5,2,1,0:T(8,128)(2,1)} fusion(bf16[2,2,2,256,256,18]{4,3,5,2,1,0:T(8,128)(2,1)} %copy.46, bf16[2,2,256]{2,1,0:T(2,128)(2,1)S(1)} %compare_convert_fusion), kind=kLoop, calls=%fused_computation.84 | loop fusion | flops 9437184 | bytes 37750784 | tf_op jit(solution)/shard_map/mul | solution.py:79
  127.0 8.4 %slice_bitcast_fusion = bf16[2,2,256,256,18]{3,2,4,1,0:T(8,128)(2,1)} fusion(bf16[2,2,2,256,256,18]{4,3,5,2,1,0:T(8,128)(2,1)} %broadcast_multiply_fusion.2), kind=kLoop, calls=%fused_computation.83 | loop fusion | bytes 18874368 | tf_op jit(solution)/shard_map/squeeze | solution.py:84
  135.4 29.6 %copy.62 = bf16[2,2,2,256,256,18]{3,5,1,2,0,4:T(8,128)(2,1)} copy(bf16[2,2,2,256,256,18]{4,3,5,2,1,0:T(8,128)(2,1)} %broadcast_multiply_fusion.2) | data formatting | bytes 37748736 | tf_op jit(solution)/shard_map/mul | solution.py:79
  165.1 15.5 %copy.50 = bf16[2,2,256,256,18]{2,4,3,1,0:T(8,128)(2,1)} copy(bf16[2,2,256,256,18]{3,2,4,1,0:T(8,128)(2,1)} %slice_bitcast_fusion) | data formatting | bytes 18874368 | tf_op jit(solution)/shard_map/squeeze | solution.py:84
  180.6 13.3 %fusion.40 = f32[2,2,256,18,18]{4,3,2,1,0:T(8,128)} fusion(bf16[2,2,256,256,18]{2,4,3,1,0:T(8,128)(2,1)} %copy.50, bf16[2,1,2,256,256,18]{3,2,5,4,1,0:T(2,128)(2,1)} %slice.35), kind=kOutput, calls=%fused_computation.80 | convolution fusion | flops 169869312 | bytes 20201472 | tf_op jit(solution)/shard_map/skbai,skbaj->skaij/dot_general | solution.py:83
  193.9 14.0 %copy.51 = f32[2,2,256,18,18]{3,4,2,1,0:T(8,128)} copy(f32[2,2,256,18,18]{4,3,2,1,0:T(8,128)} %fusion.40) | data formatting | bytes 2654208 | tf_op jit(solution)/shard_map/skbai,skbaj->skaij/dot_general | solution.py:83
  207.9 14.1 %fusion.41 = f32[2,1,2,256,18,18]{5,4,3,2,0,1:T(8,128)} fusion(f32[2,2,256,18,18]{4,3,2,1,0:T(8,128)} %fusion.40, f32[2,2,256,18,18]{3,4,2,1,0:T(8,128)} %copy.51), kind=kLoop, calls=%fused_computation.82 | loop fusion | flops 331776 | bytes 3981312 | tf_op jit(solution)/shard_map/stack | solution.py:87
  221.9 11.4 %copy.53 = f32[2,1,2,256,18,18]{3,2,5,4,1,0:T(2,128)S(1)} copy(f32[2,1,2,256,18,18]{5,4,3,2,0,1:T(8,128)} %fusion.41) | data formatting | bytes 2654208 | tf_op jit(solution)/shard_map/stack | solution.py:87
  233.4 21.8 %fusion.42 = f32[2,1,2,256,18,18]{4,5,2,0,3,1:T(8,128)} fusion(bf16[2,2,2,256,256,18]{3,5,1,2,0,4:T(8,128)(2,1)} %copy.62, bf16[2,2,2,256,256,18]{3,2,5,4,1,0:T(2,128)(2,1)} %bitcast.70), kind=kOutput, calls=%fused_computation.85 | convolution fusion | flops 339738624 | bytes 39075840 | tf_op jit(solution)/shard_map/sckbai,sckbaj->skaij/dot_general | solution.py:80
  255.1 11.6 %copy.52 = f32[2,1,2,256,18,18]{3,2,5,4,1,0:T(2,128)S(1)} copy(f32[2,1,2,256,18,18]{4,5,2,0,3,1:T(8,128)} %fusion.42) | data formatting | bytes 2654208 | tf_op jit(solution)/shard_map/stack | solution.py:87
  266.8 3.7 fusion.45
  271.6 2.4 copy.56
  278.9 60.1 %all-reduce.2.cloned.1.call-done = f32[2,2,256,324]{3,1,2,0:T(2,128)} async-done(((f32[2,2,256,324]{3,1,2,0:T(2,128)}), f32[2,2,256,324]{3,1,2,0:T(2,128)}) %all-reduce.2.cloned.1.call-update) | async-done | bytes 1327120 | tf_op jit(solution)/shard_map/psum | solution.py:93
  339.0 2.2 gather_fusion
  342.3 4.4 all-gather
  346.8 303.3 %while.14 = (s32[]{:T(128)}, f32[64,3]{0,1:T(4,128)}, f32[2,1]{0,1:T(1,128)S(1)}, s32[8]{0:T(128)S(1)}, s32[]{:T(128)}, /*index=5*/f32[64,18]{0,1:T(8,128)S(1)},...) while((s32[]{:T(128)}, f32[64,3]{0,1:T(4,128)}, ...), condition=%wide.region_5.6_spmd.clone, body=%wide.region_4.5_spmd.clone.sunk | while | flops 262103424 | bytes 21960220 | solution.py:59
  351.1 1.2 add_subtract_fusion.2
  356.1 3.7 fusion.77
  359.8 1.3 dynamic-slice_reduce_fusion.3
  361.2 18.2 %convolution_multiply_fusion.3 = f32[13824,64]{0,1:T(8,128)} fusion(f32[18,13824]{1,0:T(8,128)} %mul.712, f32[64,18]{0,1:T(8,128)S(1)} %get-tuple-element.353, f32[13824,64]{0,1:T(8,128)S(1)} %fusion.77, f32[13824]{0:T(1024)S(1)} %get-tuple-element.318, f32[13824]{0:T(1024)S(1)} %get-tuple-element.319), kind=kOutput, calls=%fused_computation.3.clone.1 | convolution fusion | flops 194641920 | bytes 8188416 | tf_op jit(solution)/shard_map/while/body/eval_jaxpr/dot_general | solution.py:42
  379.4 5.5 convolution_add_fusion.2
  389.0 1.2 add_subtract_fusion.2
  394.0 3.7 fusion.77
  397.7 1.3 dynamic-slice_reduce_fusion.3
  399.1 18.2 %convolution_multiply_fusion.3 = f32[13824,64]{0,1:T(8,128)} fusion(f32[18,13824]{1,0:T(8,128)} %mul.712, f32[64,18]{0,1:T(8,128)S(1)} %get-tuple-element.353, f32[13824,64]{0,1:T(8,128)S(1)} %fusion.77, f32[13824]{0:T(1024)S(1)} %get-tuple-element.318, f32[13824]{0:T(1024)S(1)} %get-tuple-element.319), kind=kOutput, calls=%fused_computation.3.clone.1 | convolution fusion | flops 194641920 | bytes 8188416 | tf_op jit(solution)/shard_map/while/body/eval_jaxpr/dot_general | solution.py:42
  417.3 5.5 convolution_add_fusion.2
  426.9 1.2 add_subtract_fusion.2
  429.5 1.2 mul.712
  431.9 3.7 fusion.77
  435.6 1.3 dynamic-slice_reduce_fusion.3
  436.9 18.2 %convolution_multiply_fusion.3 = f32[13824,64]{0,1:T(8,128)} fusion(f32[18,13824]{1,0:T(8,128)} %mul.712, f32[64,18]{0,1:T(8,128)S(1)} %get-tuple-element.353, f32[13824,64]{0,1:T(8,128)S(1)} %fusion.77, f32[13824]{0:T(1024)S(1)} %get-tuple-element.318, f32[13824]{0:T(1024)S(1)} %get-tuple-element.319), kind=kOutput, calls=%fused_computation.3.clone.1 | convolution fusion | flops 194641920 | bytes 8188416 | tf_op jit(solution)/shard_map/while/body/eval_jaxpr/dot_general | solution.py:42
  455.2 5.5 convolution_add_fusion.2
  464.8 1.2 add_subtract_fusion.2
  467.4 1.2 mul.712
  469.8 3.7 fusion.77
  473.5 1.3 dynamic-slice_reduce_fusion.3
  474.8 18.2 %convolution_multiply_fusion.3 = f32[13824,64]{0,1:T(8,128)} fusion(f32[18,13824]{1,0:T(8,128)} %mul.712, f32[64,18]{0,1:T(8,128)S(1)} %get-tuple-element.353, f32[13824,64]{0,1:T(8,128)S(1)} %fusion.77, f32[13824]{0:T(1024)S(1)} %get-tuple-element.318, f32[13824]{0:T(1024)S(1)} %get-tuple-element.319), kind=kOutput, calls=%fused_computation.3.clone.1 | convolution fusion | flops 194641920 | bytes 8188416 | tf_op jit(solution)/shard_map/while/body/eval_jaxpr/dot_general | solution.py:42
  493.0 5.5 convolution_add_fusion.2
  502.7 1.2 add_subtract_fusion.2
  505.2 1.2 mul.712
  507.7 3.7 fusion.77
  511.4 1.3 dynamic-slice_reduce_fusion.3
  512.7 18.2 %convolution_multiply_fusion.3 = f32[13824,64]{0,1:T(8,128)} fusion(f32[18,13824]{1,0:T(8,128)} %mul.712, f32[64,18]{0,1:T(8,128)S(1)} %get-tuple-element.353, f32[13824,64]{0,1:T(8,128)S(1)} %fusion.77, f32[13824]{0:T(1024)S(1)} %get-tuple-element.318, f32[13824]{0:T(1024)S(1)} %get-tuple-element.319), kind=kOutput, calls=%fused_computation.3.clone.1 | convolution fusion | flops 194641920 | bytes 8188416 | tf_op jit(solution)/shard_map/while/body/eval_jaxpr/dot_general | solution.py:42
  530.9 5.5 convolution_add_fusion.2
  540.6 1.2 add_subtract_fusion.2
  545.6 3.7 fusion.77
  549.3 1.3 dynamic-slice_reduce_fusion.3
  550.6 18.2 %convolution_multiply_fusion.3 = f32[13824,64]{0,1:T(8,128)} fusion(f32[18,13824]{1,0:T(8,128)} %mul.712, f32[64,18]{0,1:T(8,128)S(1)} %get-tuple-element.353, f32[13824,64]{0,1:T(8,128)S(1)} %fusion.77, f32[13824]{0:T(1024)S(1)} %get-tuple-element.318, f32[13824]{0:T(1024)S(1)} %get-tuple-element.319), kind=kOutput, calls=%fused_computation.3.clone.1 | convolution fusion | flops 194641920 | bytes 8188416 | tf_op jit(solution)/shard_map/while/body/eval_jaxpr/dot_general | solution.py:42
  568.8 5.5 convolution_add_fusion.2
  578.5 1.2 add_subtract_fusion.2
  583.5 3.7 fusion.77
  587.2 1.3 dynamic-slice_reduce_fusion.3
  588.5 18.2 %convolution_multiply_fusion.3 = f32[13824,64]{0,1:T(8,128)} fusion(f32[18,13824]{1,0:T(8,128)} %mul.712, f32[64,18]{0,1:T(8,128)S(1)} %get-tuple-element.353, f32[13824,64]{0,1:T(8,128)S(1)} %fusion.77, f32[13824]{0:T(1024)S(1)} %get-tuple-element.318, f32[13824]{0:T(1024)S(1)} %get-tuple-element.319), kind=kOutput, calls=%fused_computation.3.clone.1 | convolution fusion | flops 194641920 | bytes 8188416 | tf_op jit(solution)/shard_map/while/body/eval_jaxpr/dot_general | solution.py:42
  606.7 5.5 convolution_add_fusion.2
  616.3 1.2 add_subtract_fusion.2
  621.4 3.7 fusion.77
  625.1 1.3 dynamic-slice_reduce_fusion.3
  626.4 18.2 %convolution_multiply_fusion.3 = f32[13824,64]{0,1:T(8,128)} fusion(f32[18,13824]{1,0:T(8,128)} %mul.712, f32[64,18]{0,1:T(8,128)S(1)} %get-tuple-element.353, f32[13824,64]{0,1:T(8,128)S(1)} %fusion.77, f32[13824]{0:T(1024)S(1)} %get-tuple-element.318, f32[13824]{0:T(1024)S(1)} %get-tuple-element.319), kind=kOutput, calls=%fused_computation.3.clone.1 | convolution fusion | flops 194641920 | bytes 8188416 | tf_op jit(solution)/shard_map/while/body/eval_jaxpr/dot_general | solution.py:42
  644.6 5.5 convolution_add_fusion.2
  650.2 4.9 psum.15
  (259 shorter events, 62.5 us)
Async XLA Ops:
  8.0 267.3 %copy-start = (s32[512]{0:T(512)S(1)}, s32[512]{0:T(512)}, u32[]{:S(2)}) copy-start(s32[512]{0:T(512)} %param.15) | copy-start | bytes 6148
  8.0 266.3 %sort.19.cloned.1.call-start = ((), (), s32[]{:S(2)}) async-start(), calls=%async_computation.1 | async-start | bytes 12320 | tf_op jit(solution)/shard_map/jit(argsort)/sort | solution.py:91
  9.9 329.0 %all-reduce.2.cloned.1.call-start = ((), (), s32[]{:S(2)}) async-start(), calls=%async_computation | async-start | bytes 3145728 | tf_op jit(solution)/shard_map/psum | solution.py:93
  101.1 9.1 %copy-start.8 = (s32[2,2]{1,0:T(2,128)S(1)}, s32[2,2]{1,0:T(2,128)}, u32[]{:S(2)}) copy-start(s32[2,2]{1,0:T(2,128)} %param.12) | copy-start | bytes 52
  255.1 11.6 %copy-start.9 = (f32[2]{0:T(128)S(1)}, f32[2]{0:T(128)}, u32[]{:S(2)}) copy-start(f32[2]{0:T(128)} %param.13) | copy-start | bytes 28
  270.5 3.6 copy-start.10
  270.5 3.6 copy-start.4
  270.6 3.6 copy-start.7
  347.0 1.2 copy-start.11
  347.0 6.4 copy-start.5
  355.3 0.8 copy-start.1
  356.1 3.7 copy-start.2
  356.1 3.7 copy-start.3
  379.4 5.5 copy-start.6
  379.4 5.5 copy-start.12
  384.9 1.2 copy-start.11
  384.9 6.4 copy-start.5
  393.2 0.8 copy-start.1
  394.0 3.7 copy-start.2
  394.0 3.7 copy-start.3
  417.3 5.5 copy-start.6
  417.3 5.5 copy-start.12
  422.8 1.2 copy-start.11
  422.8 6.4 copy-start.5
  431.0 0.8 copy-start.1
  431.9 3.7 copy-start.2
  431.9 3.7 copy-start.3
  455.2 5.5 copy-start.6
  455.2 5.5 copy-start.12
  460.7 1.2 copy-start.11
  460.7 6.4 copy-start.5
  468.9 0.8 copy-start.1
  469.8 3.7 copy-start.2
  469.8 3.7 copy-start.3
  493.0 5.5 copy-start.6
  493.0 5.5 copy-start.12
  498.6 1.2 copy-start.11
  498.6 6.4 copy-start.5
  506.8 0.8 copy-start.1
  507.7 3.7 copy-start.2
  507.7 3.7 copy-start.3
  530.9 5.5 copy-start.6
  530.9 5.5 copy-start.12
  536.5 1.2 copy-start.11
  536.5 6.4 copy-start.5
  544.7 0.8 copy-start.1
  545.6 3.7 copy-start.2
  545.6 3.7 copy-start.3
  568.8 5.5 copy-start.6
  568.8 5.5 copy-start.12
  574.4 1.2 copy-start.11
  574.4 6.4 copy-start.5
  582.6 0.8 copy-start.1
  583.5 3.7 copy-start.2
  583.5 3.7 copy-start.3
  606.7 5.5 copy-start.6
  606.7 5.5 copy-start.12
  612.3 1.2 copy-start.11
  612.3 6.4 copy-start.5
  620.5 0.8 copy-start.1
  621.3 3.7 copy-start.2
  621.4 3.7 copy-start.3
  644.6 5.5 copy-start.6
  644.6 5.5 copy-start.12
Sparse Core Ops, SparseCore 0:
  11.7 2.2 sort.21.cloned.1.call-done
  (1 shorter events, 0.0 us)
Sparse Core Ops, SparseCore 1:
  274.1 64.8 all-reduce.1
where the time goes:
time: 668 us; the launch traced here: 663 us
  matrix products  255 us (38%)
  local copies, waits for them, and re-layouts  234 us (35%)
  other arithmetic  83.3 us (12%)
  waiting for transfers between devices  60.1 us (9%)
  between operations  15.7 us (2%)
  blocking collectives  9.31 us (1%)
    dot_general x8, matrix products, force_block(): smooth = jnp.dot(moments, form_table, precision=highest)  146 us
    psum x1, waiting for transfers between devices, shards(): summed = lax.psum(density_local, ('ka', 'ba'))  60.1 us
    unnamed x19, local copies, waits for them, and re-layouts  47.3 us
    reshape x1, local copies, waits for them, and re-layouts, shards(): coefficients.reshape(spin_count, complex_parts, kcount, bcount, atoms_blk...  45.4 us
    dot_general x8, matrix products, force_block(): return jnp.dot(smooth * wave_term, vectors, precision=highest)  44.3 us
    mul x1, local copies, waits for them, and re-layouts, shards(): masked = values * band_mask[:, None, :, :, None, None]  29.6 us
    dot_general x8, matrix products, force_block(): phases = jnp.dot(places, vectors.T, precision=highest)  29.6 us
    squeeze x2, local copies, waits for them, and re-layouts, shards(): masked[:, 1]  23.9 us
  transfers between devices with their start and end apart: 1, of which 1 were waited for; matrix products, arithmetic and copies ran while one was open for 1% of the time, Pallas kernels for 0%

commit v1 on v0

--- a/solution.py
+++ b/solution.py
@@ -90,7 +90,7 @@
     )
     ranking = jnp.argsort(owner_map.reshape(-1, atoms_blk), axis=1, stable=True)
     own_ranks = lax.dynamic_slice_in_dim(ranking, owner_index * per_owner, per_owner, 1)
-    summed = lax.psum(density_local, ("ka", "ba"))
+    summed = jnp.sum(lax.all_gather(density_local, ("ka", "ba")), axis=0)
     own_rows = lax.dynamic_index_in_dim(own_ranks, group_index, 0, keepdims=False)
     own_density = jnp.take(summed, own_rows, axis=2)
     block_count = own_ranks.shape[0]

time: 668 us -> 716 us (1.072)
  waiting for transfers between devices: 60.1 us -> 98.4 us
  other arithmetic: 83.3 us -> 94.1 us
    all_gather x0 -> x1, waiting for transfers between devices: none -> 98.4 us  [shards(): summed = jnp.sum(lax.all_gather(density_local, ('ka', 'ba')), axis=0)]
    psum x1 -> x0, waiting for transfers between devices: 60.1 us -> none  [shards(): summed = lax.psum(density_local, ('ka', 'ba'))]
    reduce_sum x0 -> x1, other arithmetic: none -> 10.8 us  [shards(): summed = jnp.sum(lax.all_gather(density_local, ('ka', 'ba')), axis=0)]
where the time goes in v1:
time: 716 us; the launch traced here: 711 us
  matrix products  255 us (36%)
  local copies, waits for them, and re-layouts  233 us (33%)
  waiting for transfers between devices  98.4 us (14%)
  other arithmetic  94.1 us (13%)
  between operations  15.8 us (2%)
  blocking collectives  9.31 us (1%)
    dot_general x8, matrix products, force_block(): smooth = jnp.dot(moments, form_table, precision=highest)  146 us
    all_gather x1, waiting for transfers between devices, shards(): summed = jnp.sum(lax.all_gather(density_local, ('ka', 'ba')), axis=0)  98.4 us
    unnamed x19, local copies, waits for them, and re-layouts  47.3 us
    reshape x1, local copies, waits for them, and re-layouts, shards(): coefficients.reshape(spin_count, complex_parts, kcount, bcount, atoms_blk...  45.4 us
    dot_general x8, matrix products, force_block(): return jnp.dot(smooth * wave_term, vectors, precision=highest)  44.2 us
    mul x1, local copies, waits for them, and re-layouts, shards(): masked = values * band_mask[:, None, :, :, None, None]  29.6 us
    dot_general x8, matrix products, force_block(): phases = jnp.dot(places, vectors.T, precision=highest)  29.6 us
    squeeze x2, local copies, waits for them, and re-layouts, shards(): masked[:, 1]  23.9 us
  transfers between devices with their start and end apart: 1, of which 1 were waited for; matrix products, arithmetic and copies ran while one was open for 1% of the time, Pallas kernels for 0%

profile of v1, /device:TPU:0, one launch (start us, length us, event | category | flops | bytes accessed | tf_op | source)
XLA Modules:
  0.0 710.6 jit_solution(487447894653610051)
XLA Ops:
  8.1 1.3 reshape.500
  10.0 45.7 %copy.44 = bf16[2,2,2,256,4608]{3,2,4,1,0:T(2,128)(2,1)} copy(bf16[2,2,2,256,4608]{4,3,2,1,0:T(8,128)(2,1)} %param.11) | data formatting | bytes 37748736 | tf_op args[0]
  55.7 45.4 %copy.45 = bf16[2,2,2,256,256,18]{4,3,5,2,1,0:T(8,128)(2,1)} copy(bf16[2,2,2,256,256,18]{3,2,5,4,1,0:T(2,128)(2,1)} %bitcast.68) | data formatting | bytes 37748736 | tf_op jit(solution)/shard_map/reshape | solution.py:78
  101.1 9.1 %slice.35 = bf16[2,1,2,256,256,18]{3,2,5,4,1,0:T(2,128)(2,1)} slice(bf16[2,2,2,256,256,18]{3,2,5,4,1,0:T(2,128)(2,1)} %bitcast.69), slice={[0:2], [0:1], [0:2], [0:256], [0:256], [0:18]} | slice | bytes 18874368 | tf_op jit(solution)/shard_map/slice | solution.py:84
  110.3 16.7 %broadcast_multiply_fusion.2 = bf16[2,2,2,256,256,18]{4,3,5,2,1,0:T(8,128)(2,1)} fusion(bf16[2,2,2,256,256,18]{4,3,5,2,1,0:T(8,128)(2,1)} %copy.45, bf16[2,2,256]{2,1,0:T(2,128)(2,1)S(1)} %compare_convert_fusion), kind=kLoop, calls=%fused_computation.84 | loop fusion | flops 9437184 | bytes 37750784 | tf_op jit(solution)/shard_map/mul | solution.py:79
  127.0 8.4 %slice_bitcast_fusion = bf16[2,2,256,256,18]{3,2,4,1,0:T(8,128)(2,1)} fusion(bf16[2,2,2,256,256,18]{4,3,5,2,1,0:T(8,128)(2,1)} %broadcast_multiply_fusion.2), kind=kLoop, calls=%fused_computation.83 | loop fusion | bytes 18874368 | tf_op jit(solution)/shard_map/squeeze | solution.py:84
  135.4 29.6 %copy.61 = bf16[2,2,2,256,256,18]{3,5,1,2,0,4:T(8,128)(2,1)} copy(bf16[2,2,2,256,256,18]{4,3,5,2,1,0:T(8,128)(2,1)} %broadcast_multiply_fusion.2) | data formatting | bytes 37748736 | tf_op jit(solution)/shard_map/mul | solution.py:79
  165.1 15.5 %copy.49 = bf16[2,2,256,256,18]{2,4,3,1,0:T(8,128)(2,1)} copy(bf16[2,2,256,256,18]{3,2,4,1,0:T(8,128)(2,1)} %slice_bitcast_fusion) | data formatting | bytes 18874368 | tf_op jit(solution)/shard_map/squeeze | solution.py:84
  180.6 13.3 %fusion.40 = f32[2,2,256,18,18]{4,3,2,1,0:T(8,128)} fusion(bf16[2,2,256,256,18]{2,4,3,1,0:T(8,128)(2,1)} %copy.49, bf16[2,1,2,256,256,18]{3,2,5,4,1,0:T(2,128)(2,1)} %slice.35), kind=kOutput, calls=%fused_computation.80 | convolution fusion | flops 169869312 | bytes 20201472 | tf_op jit(solution)/shard_map/skbai,skbaj->skaij/dot_general | solution.py:83
  193.9 14.0 %copy.50 = f32[2,2,256,18,18]{3,4,2,1,0:T(8,128)} copy(f32[2,2,256,18,18]{4,3,2,1,0:T(8,128)} %fusion.40) | data formatting | bytes 2654208 | tf_op jit(solution)/shard_map/skbai,skbaj->skaij/dot_general | solution.py:83
  207.9 14.1 %fusion.41 = f32[2,1,2,256,18,18]{5,4,3,2,0,1:T(8,128)} fusion(f32[2,2,256,18,18]{4,3,2,1,0:T(8,128)} %fusion.40, f32[2,2,256,18,18]{3,4,2,1,0:T(8,128)} %copy.50), kind=kLoop, calls=%fused_computation.82 | loop fusion | flops 331776 | bytes 3981312 | tf_op jit(solution)/shard_map/stack | solution.py:87
  221.9 11.4 %copy.52 = f32[2,1,2,256,18,18]{3,2,5,4,1,0:T(2,128)S(1)} copy(f32[2,1,2,256,18,18]{5,4,3,2,0,1:T(8,128)} %fusion.41) | data formatting | bytes 2654208 | tf_op jit(solution)/shard_map/stack | solution.py:87
  233.4 21.8 %fusion.42 = f32[2,1,2,256,18,18]{4,5,2,0,3,1:T(8,128)} fusion(bf16[2,2,2,256,256,18]{3,5,1,2,0,4:T(8,128)(2,1)} %copy.61, bf16[2,2,2,256,256,18]{3,2,5,4,1,0:T(2,128)(2,1)} %bitcast.70), kind=kOutput, calls=%fused_computation.85 | convolution fusion | flops 339738624 | bytes 39075840 | tf_op jit(solution)/shard_map/sckbai,sckbaj->skaij/dot_general | solution.py:80
  255.1 11.6 %copy.51 = f32[2,1,2,256,18,18]{3,2,5,4,1,0:T(2,128)S(1)} copy(f32[2,1,2,256,18,18]{4,5,2,0,3,1:T(8,128)} %fusion.42) | data formatting | bytes 2654208 | tf_op jit(solution)/shard_map/stack | solution.py:87
  266.8 3.7 fusion.45
  270.6 2.1 copy.54
  277.5 98.4 %all-gather.3.cloned.1.call-done = f32[8,2,2,256,324]{3,2,4,1,0:T(2,128)} async-done(((f32[1,2,2,256,324]{3,2,4,1,0:T(2,128)}), f32[8,2,2,256,324]{3,2,4,1,0:T(2,128)}) %all-gather.3.cloned.1.call-update) | async-done | bytes 10616848 | tf_op jit(solution)/shard_map/all_gather | solution.py:93
  375.9 10.8 %reduce_sum.28 = f32[2,2,256,324]{2,1,3,0:T(2,128)S(1)} reduce(f32[8,2,2,256,324]{3,2,4,1,0:T(2,128)} %all-gather.3.cloned.1.call-done, f32[]{:T(128)} %constant.178.clone.1), dimensions={0}, to_apply=%region_2.3 | reduce | flops 2322432 | bytes 11943940 | tf_op jit(solution)/shard_map/reduce_sum | solution.py:93
  386.7 1.3 copy.55
  390.0 4.4 all-gather
  394.5 303.1 %while.14 = (s32[]{:T(128)}, f32[64,3]{0,1:T(4,128)}, f32[2,1]{0,1:T(1,128)S(1)}, s32[8]{0:T(128)S(1)}, s32[]{:T(128)}, /*index=5*/f32[64,18]{0,1:T(8,128)S(1)},...) while((s32[]{:T(128)}, f32[64,3]{0,1:T(4,128)}, ...), condition=%wide.region_5.6_spmd.clone, body=%wide.region_4.5_spmd.clone.sunk | while | flops 262103424 | bytes 21960220 | solution.py:59
  398.7 1.2 add_subtract_fusion.2
  403.8 3.7 fusion.77
  407.5 1.3 dynamic-slice_reduce_fusion.3
  408.8 18.2 %convolution_multiply_fusion.3 = f32[13824,64]{0,1:T(8,128)} fusion(f32[18,13824]{1,0:T(8,128)} %mul.712, f32[64,18]{0,1:T(8,128)S(1)} %get-tuple-element.353, f32[13824,64]{0,1:T(8,128)S(1)} %fusion.77, f32[13824]{0:T(1024)S(1)} %get-tuple-element.318, f32[13824]{0:T(1024)S(1)} %get-tuple-element.319), kind=kOutput, calls=%fused_computation.3.clone.1 | convolution fusion | flops 194641920 | bytes 8188416 | tf_op jit(solution)/shard_map/while/body/eval_jaxpr/dot_general | solution.py:42
  427.0 5.5 convolution_add_fusion.2
  436.6 1.2 add_subtract_fusion.2
  439.2 1.2 mul.712
  441.6 3.7 fusion.77
  445.4 1.3 dynamic-slice_reduce_fusion.3
  446.7 18.2 %convolution_multiply_fusion.3 = f32[13824,64]{0,1:T(8,128)} fusion(f32[18,13824]{1,0:T(8,128)} %mul.712, f32[64,18]{0,1:T(8,128)S(1)} %get-tuple-element.353, f32[13824,64]{0,1:T(8,128)S(1)} %fusion.77, f32[13824]{0:T(1024)S(1)} %get-tuple-element.318, f32[13824]{0:T(1024)S(1)} %get-tuple-element.319), kind=kOutput, calls=%fused_computation.3.clone.1 | convolution fusion | flops 194641920 | bytes 8188416 | tf_op jit(solution)/shard_map/while/body/eval_jaxpr/dot_general | solution.py:42
  464.9 5.5 convolution_add_fusion.2
  474.5 1.2 add_subtract_fusion.2
  479.5 3.7 fusion.77
  483.2 1.3 dynamic-slice_reduce_fusion.3
  484.5 18.2 %convolution_multiply_fusion.3 = f32[13824,64]{0,1:T(8,128)} fusion(f32[18,13824]{1,0:T(8,128)} %mul.712, f32[64,18]{0,1:T(8,128)S(1)} %get-tuple-element.353, f32[13824,64]{0,1:T(8,128)S(1)} %fusion.77, f32[13824]{0:T(1024)S(1)} %get-tuple-element.318, f32[13824]{0:T(1024)S(1)} %get-tuple-element.319), kind=kOutput, calls=%fused_computation.3.clone.1 | convolution fusion | flops 194641920 | bytes 8188416 | tf_op jit(solution)/shard_map/while/body/eval_jaxpr/dot_general | solution.py:42
  502.7 5.5 convolution_add_fusion.2
  512.3 1.2 add_subtract_fusion.2
  517.3 3.7 fusion.77
  521.1 1.3 dynamic-slice_reduce_fusion.3
  522.4 18.2 %convolution_multiply_fusion.3 = f32[13824,64]{0,1:T(8,128)} fusion(f32[18,13824]{1,0:T(8,128)} %mul.712, f32[64,18]{0,1:T(8,128)S(1)} %get-tuple-element.353, f32[13824,64]{0,1:T(8,128)S(1)} %fusion.77, f32[13824]{0:T(1024)S(1)} %get-tuple-element.318, f32[13824]{0:T(1024)S(1)} %get-tuple-element.319), kind=kOutput, calls=%fused_computation.3.clone.1 | convolution fusion | flops 194641920 | bytes 8188416 | tf_op jit(solution)/shard_map/while/body/eval_jaxpr/dot_general | solution.py:42
  540.6 5.5 convolution_add_fusion.2
  550.2 1.2 add_subtract_fusion.2
  552.8 1.2 mul.712
  555.2 3.7 fusion.77
  558.9 1.3 dynamic-slice_reduce_fusion.3
  560.3 18.2 %convolution_multiply_fusion.3 = f32[13824,64]{0,1:T(8,128)} fusion(f32[18,13824]{1,0:T(8,128)} %mul.712, f32[64,18]{0,1:T(8,128)S(1)} %get-tuple-element.353, f32[13824,64]{0,1:T(8,128)S(1)} %fusion.77, f32[13824]{0:T(1024)S(1)} %get-tuple-element.318, f32[13824]{0:T(1024)S(1)} %get-tuple-element.319), kind=kOutput, calls=%fused_computation.3.clone.1 | convolution fusion | flops 194641920 | bytes 8188416 | tf_op jit(solution)/shard_map/while/body/eval_jaxpr/dot_general | solution.py:42
  578.5 5.5 convolution_add_fusion.2
  588.0 1.2 add_subtract_fusion.2
  593.1 3.7 fusion.77
  596.8 1.3 dynamic-slice_reduce_fusion.3
  598.1 18.2 %convolution_multiply_fusion.3 = f32[13824,64]{0,1:T(8,128)} fusion(f32[18,13824]{1,0:T(8,128)} %mul.712, f32[64,18]{0,1:T(8,128)S(1)} %get-tuple-element.353, f32[13824,64]{0,1:T(8,128)S(1)} %fusion.77, f32[13824]{0:T(1024)S(1)} %get-tuple-element.318, f32[13824]{0:T(1024)S(1)} %get-tuple-element.319), kind=kOutput, calls=%fused_computation.3.clone.1 | convolution fusion | flops 194641920 | bytes 8188416 | tf_op jit(solution)/shard_map/while/body/eval_jaxpr/dot_general | solution.py:42
  616.3 5.5 convolution_add_fusion.2
  625.9 1.2 add_subtract_fusion.2
  630.9 3.7 fusion.77
  634.7 1.3 dynamic-slice_reduce_fusion.3
  636.0 18.2 %convolution_multiply_fusion.3 = f32[13824,64]{0,1:T(8,128)} fusion(f32[18,13824]{1,0:T(8,128)} %mul.712, f32[64,18]{0,1:T(8,128)S(1)} %get-tuple-element.353, f32[13824,64]{0,1:T(8,128)S(1)} %fusion.77, f32[13824]{0:T(1024)S(1)} %get-tuple-element.318, f32[13824]{0:T(1024)S(1)} %get-tuple-element.319), kind=kOutput, calls=%fused_computation.3.clone.1 | convolution fusion | flops 194641920 | bytes 8188416 | tf_op jit(solution)/shard_map/while/body/eval_jaxpr/dot_general | solution.py:42
  654.2 5.5 convolution_add_fusion.2
  663.8 1.2 add_subtract_fusion.2
  668.8 3.7 fusion.77
  672.5 1.3 dynamic-slice_reduce_fusion.3
  673.8 18.2 %convolution_multiply_fusion.3 = f32[13824,64]{0,1:T(8,128)} fusion(f32[18,13824]{1,0:T(8,128)} %mul.712, f32[64,18]{0,1:T(8,128)S(1)} %get-tuple-element.353, f32[13824,64]{0,1:T(8,128)S(1)} %fusion.77, f32[13824]{0:T(1024)S(1)} %get-tuple-element.318, f32[13824]{0:T(1024)S(1)} %get-tuple-element.319), kind=kOutput, calls=%fused_computation.3.clone.1 | convolution fusion | flops 194641920 | bytes 8188416 | tf_op jit(solution)/shard_map/while/body/eval_jaxpr/dot_general | solution.py:42
  692.0 5.5 convolution_add_fusion.2
  697.6 4.9 psum.7
  (260 shorter events, 63.5 us)
Async XLA Ops:
  8.0 265.9 %copy-start = (s32[512]{0:T(512)S(1)}, s32[512]{0:T(512)}, u32[]{:S(2)}) copy-start(s32[512]{0:T(512)} %param.15) | copy-start | bytes 6148
  8.0 265.0 %sort.19.cloned.1.call-start = ((), (), s32[]{:S(2)}) async-start(), calls=%async_computation.1 | async-start | bytes 12320 | tf_op jit(solution)/shard_map/jit(argsort)/sort | solution.py:91
  9.9 365.9 %all-gather.3.cloned.1.call-start = ((), (), s32[]{:S(2)}) async-start(), calls=%async_computation | async-start | bytes 11943936 | tf_op jit(solution)/shard_map/all_gather | solution.py:93
  101.1 9.1 %copy-start.8 = (s32[2,2]{1,0:T(2,128)S(1)}, s32[2,2]{1,0:T(2,128)}, u32[]{:S(2)}) copy-start(s32[2,2]{1,0:T(2,128)} %param.12) | copy-start | bytes 52
  255.1 11.6 %copy-start.9 = (f32[2]{0:T(128)S(1)}, f32[2]{0:T(128)}, u32[]{:S(2)}) copy-start(f32[2]{0:T(128)} %param.13) | copy-start | bytes 28
  266.8 5.9 copy-start.4
  266.8 6.0 copy-start.7
  270.6 2.4 copy-start.10
  394.7 7.8 %copy-start.5 = (f32[2,1]{0,1:T(1,128)}, f32[2,1]{0,1:T(1,128)S(1)}, u32[]{:S(2)}) copy-start(f32[2,1]{0,1:T(1,128)S(1)} %get-tuple-element.350) | copy-start | bytes 28 | tf_op jit(solution)/shard_map/while
  394.7 7.8 %copy-start.11 = (s32[8]{0:T(128)}, s32[8]{0:T(128)S(1)}, u32[]{:S(2)}) copy-start(s32[8]{0:T(128)S(1)} %get-tuple-element.351) | copy-start | bytes 100 | tf_op jit(solution)/shard_map/while
  402.9 0.8 copy-start.1
  403.7 3.7 copy-start.2
  403.7 3.7 copy-start.3
  427.0 5.5 copy-start.6
  427.0 5.5 copy-start.12
  432.5 7.8 %copy-start.5 = (f32[2,1]{0,1:T(1,128)}, f32[2,1]{0,1:T(1,128)S(1)}, u32[]{:S(2)}) copy-start(f32[2,1]{0,1:T(1,128)S(1)} %get-tuple-element.350) | copy-start | bytes 28 | tf_op jit(solution)/shard_map/while
  432.5 7.8 %copy-start.11 = (s32[8]{0:T(128)}, s32[8]{0:T(128)S(1)}, u32[]{:S(2)}) copy-start(s32[8]{0:T(128)S(1)} %get-tuple-element.351) | copy-start | bytes 100 | tf_op jit(solution)/shard_map/while
  440.8 0.8 copy-start.1
  441.6 3.7 copy-start.2
  441.6 3.7 copy-start.3
  464.9 5.5 copy-start.6
  464.9 5.5 copy-start.12
  470.4 7.8 %copy-start.5 = (f32[2,1]{0,1:T(1,128)}, f32[2,1]{0,1:T(1,128)S(1)}, u32[]{:S(2)}) copy-start(f32[2,1]{0,1:T(1,128)S(1)} %get-tuple-element.350) | copy-start | bytes 28 | tf_op jit(solution)/shard_map/while
  470.4 7.8 %copy-start.11 = (s32[8]{0:T(128)}, s32[8]{0:T(128)S(1)}, u32[]{:S(2)}) copy-start(s32[8]{0:T(128)S(1)} %get-tuple-element.351) | copy-start | bytes 100 | tf_op jit(solution)/shard_map/while
  478.6 0.8 copy-start.1
  479.5 3.7 copy-start.2
  479.5 3.7 copy-start.3
  502.7 5.5 copy-start.6
  502.7 5.5 copy-start.12
  508.3 7.8 %copy-start.5 = (f32[2,1]{0,1:T(1,128)}, f32[2,1]{0,1:T(1,128)S(1)}, u32[]{:S(2)}) copy-start(f32[2,1]{0,1:T(1,128)S(1)} %get-tuple-element.350) | copy-start | bytes 28 | tf_op jit(solution)/shard_map/while
  508.3 7.8 %copy-start.11 = (s32[8]{0:T(128)}, s32[8]{0:T(128)S(1)}, u32[]{:S(2)}) copy-start(s32[8]{0:T(128)S(1)} %get-tuple-element.351) | copy-start | bytes 100 | tf_op jit(solution)/shard_map/while
  516.5 0.8 copy-start.1
  517.3 3.7 copy-start.2
  517.3 3.7 copy-start.3
  540.6 5.5 copy-start.6
  540.6 5.5 copy-start.12
  546.1 7.8 %copy-start.5 = (f32[2,1]{0,1:T(1,128)}, f32[2,1]{0,1:T(1,128)S(1)}, u32[]{:S(2)}) copy-start(f32[2,1]{0,1:T(1,128)S(1)} %get-tuple-element.350) | copy-start | bytes 28 | tf_op jit(solution)/shard_map/while
  546.1 7.8 %copy-start.11 = (s32[8]{0:T(128)}, s32[8]{0:T(128)S(1)}, u32[]{:S(2)}) copy-start(s32[8]{0:T(128)S(1)} %get-tuple-element.351) | copy-start | bytes 100 | tf_op jit(solution)/shard_map/while
  554.4 0.8 copy-start.1
  555.2 3.7 copy-start.2
  555.2 3.7 copy-start.3
  578.5 5.5 copy-start.6
  578.5 5.5 copy-start.12
  584.0 7.8 %copy-start.5 = (f32[2,1]{0,1:T(1,128)}, f32[2,1]{0,1:T(1,128)S(1)}, u32[]{:S(2)}) copy-start(f32[2,1]{0,1:T(1,128)S(1)} %get-tuple-element.350) | copy-start | bytes 28 | tf_op jit(solution)/shard_map/while
  584.0 7.8 %copy-start.11 = (s32[8]{0:T(128)}, s32[8]{0:T(128)S(1)}, u32[]{:S(2)}) copy-start(s32[8]{0:T(128)S(1)} %get-tuple-element.351) | copy-start | bytes 100 | tf_op jit(solution)/shard_map/while
  592.2 0.8 copy-start.1
  593.0 3.7 copy-start.2
  593.0 3.7 copy-start.3
  616.3 5.5 copy-start.6
  616.3 5.5 copy-start.12
  621.8 7.8 %copy-start.5 = (f32[2,1]{0,1:T(1,128)}, f32[2,1]{0,1:T(1,128)S(1)}, u32[]{:S(2)}) copy-start(f32[2,1]{0,1:T(1,128)S(1)} %get-tuple-element.350) | copy-start | bytes 28 | tf_op jit(solution)/shard_map/while
  621.8 7.8 %copy-start.11 = (s32[8]{0:T(128)}, s32[8]{0:T(128)S(1)}, u32[]{:S(2)}) copy-start(s32[8]{0:T(128)S(1)} %get-tuple-element.351) | copy-start | bytes 100 | tf_op jit(solution)/shard_map/while
  630.1 0.8 copy-start.1
  630.9 3.7 copy-start.2
  630.9 3.7 copy-start.3
  654.2 5.5 copy-start.6
  654.2 5.5 copy-start.12
  659.7 7.8 %copy-start.5 = (f32[2,1]{0,1:T(1,128)}, f32[2,1]{0,1:T(1,128)S(1)}, u32[]{:S(2)}) copy-start(f32[2,1]{0,1:T(1,128)S(1)} %get-tuple-element.350) | copy-start | bytes 28 | tf_op jit(solution)/shard_map/while
  659.7 7.8 %copy-start.11 = (s32[8]{0:T(128)}, s32[8]{0:T(128)S(1)}, u32[]{:S(2)}) copy-start(s32[8]{0:T(128)S(1)} %get-tuple-element.351) | copy-start | bytes 100 | tf_op jit(solution)/shard_map/while
  667.9 0.8 copy-start.1
  668.8 3.7 copy-start.2
  668.8 3.7 copy-start.3
  692.0 5.5 copy-start.6
  692.0 5.5 copy-start.12
Sparse Core Ops, SparseCore 0:
  11.7 2.2 sort.21.cloned.1.call-done
  (1 shorter events, 0.0 us)
Sparse Core Ops, SparseCore 1:
  272.8 103.0 all-gather.2
